TPU v7x, 32 devices: a whole 2x2x4 slice. The times are simulated.
32 devices in a mesh: groups: 2 (over y), hx: 16 (over z, x, core).
Axes of the slice: x: 2, y: 2, z: 4, core: 2. Of those that a mesh axis runs over, the one named last changes fastest.
Arguments:
- tokens: bfloat16 [32, 8192], P(('groups', 'hx')), parts along dimension 0, may hold values from -6 to 6
- gate_codes: bfloat16 [8192, 26624], P(None, 'hx'), may hold values from -8 to 7, as said below
- gate_scales: float32 [64, 26624], P(None, 'hx'), may hold values from 0.00077339803 to 0.00773398
- up_codes: bfloat16 [8192, 26624], P(None, 'hx'), may hold values from -8 to 7, as said below
- up_scales: float32 [64, 26624], P(None, 'hx'), may hold values from 0.00077339803 to 0.00773398
- down_codes: bfloat16 [26624, 8192], P('hx'), may hold values from -8 to 7, as said below
- down_scales: float32 [8192], replicated, may hold values from 0.00061286293 to 0.006128629
- hadamard: int32 [52, 52], replicated, may hold values from -1 to 1, as said below
Outputs:
- mixed: bfloat16 [32, 8192], P(('groups', 'hx')), parts along dimension 0
There are 2 independent parts, one for each index of `groups`. A program takes and returns all parts, laid end to end along the dimension named above; an argument that names none is the same for every part. Nothing has to cross between parts.
Inputs may be any that keep to these rules, and one draw needn't show every extreme that they name: `gate_codes`: whole numbers. `up_codes`: whole numbers. `down_codes`: whole numbers. `hadamard`: a Hadamard matrix: every entry is -1 or 1 and any two rows are orthogonal.
All inputs are finite; a program needn't handle non-finite values.
Results may differ from a plain program's by a relative error of at most 0.015.
Values may be sent and summed in bfloat16 or wider, within the bound.
A program may use at most 192 MiB of HBM per device.

v0:
```python
import functools
import math

import jax
import jax.numpy as jnp
from jax import lax
from jax.experimental import pallas as pl
from jax.experimental.pallas import tpu as pltpu
from jax.sharding import PartitionSpec as P

HA = 512
HB = 52
FF = 26624


def sylvester(size):
    index_vec = jnp.arange(size, dtype=jnp.int32)
    parity = jnp.zeros((size, size), jnp.int32)
    for level in range(max(size.bit_length() - 1, 0)):
        left_bits = jnp.right_shift(index_vec[:, None], level) & 1
        right_bits = jnp.right_shift(index_vec[None, :], level) & 1
        parity = parity + left_bits * right_bits
    return (1 - 2 * (parity % 2)).astype(jnp.float32)


def dequantize(codes, scales):
    row_total, col_total = codes.shape
    group_total = scales.shape[0]
    grouped = codes.astype(jnp.float32).reshape(group_total, row_total // group_total, col_total)
    return (grouped * scales[:, None, :]).reshape(row_total, col_total).astype(jnp.bfloat16)


LANES = 128
ROWS = 16
CHUNK_GROUPS = 4
SLOTS = 7


def kernel(
    n, tok_ref, gate_ref, gscale_ref, up_ref, uscale_ref, down_ref, dscale_ref, had_ref,
    out_ref,
    ring, gs, us, down, ds, had, corner, table, local, tok_row, tok_f32, tok_out_buf, tok, stage, lhs, acc, zbuf, recv_z, rbuf, rot, part, sendbuf, recv_c,
    ring_sem, load_sem, down_sem, tok_send, tok_recv, z_send, z_recv, r_send, r_recv, c_send, c_recv,
):
    me = lax.axis_index("hx")
    pieces = tok.shape[0]
    units = gate_ref.shape[1]
    owners = units // LANES
    chunk_rows = ring.shape[2]
    chunks = gate_ref.shape[0] // chunk_rows
    down_chunks, _, down_cols = down.shape
    out_pieces = recv_c.shape[0]
    peers = [lax.rem(me + step, n) for step in range(1, n)]

    def gate_copy(c, slot):
        rows = pl.ds(pl.multiple_of(c * chunk_rows, chunk_rows), chunk_rows)
        return pltpu.make_async_copy(gate_ref.at[rows], ring.at[slot, 0], ring_sem.at[slot, 0])

    def up_copy(c, slot):
        rows = pl.ds(pl.multiple_of(c * chunk_rows, chunk_rows), chunk_rows)
        return pltpu.make_async_copy(up_ref.at[rows], ring.at[slot, 1], ring_sem.at[slot, 1])

    def down_copy(c):
        cols = pl.ds(pl.multiple_of(c * down_cols, down_cols), down_cols)
        return pltpu.make_async_copy(down_ref.at[:, cols], down.at[c], down_sem.at[c])

    loads = [
        pltpu.make_async_copy(src, dst, load_sem.at[i])
        for i, (src, dst) in enumerate(
            ((tok_ref, tok_row), (had_ref, had), (dscale_ref, ds), (gscale_ref, gs), (uscale_ref, us))
        )
    ]

    barrier = pltpu.get_barrier_semaphore()
    for peer in peers:
        pl.semaphore_signal(barrier, inc=1, device_id={"hx": peer}, device_id_type=pl.DeviceIdType.MESH)
    for copy in loads:
        copy.start()
    for c in range(SLOTS):
        gate_copy(c, c).start()
        up_copy(c, c).start()
    loads[0].wait()
    row = tok_row[...].astype(jnp.float32)
    for k in range(pieces * ROWS):
        tok_f32[k : k + 1, :] = row[:, k * LANES : (k + 1) * LANES]
    tok_out_buf[...] = tok_f32[...].astype(jnp.bfloat16)
    for p in range(pieces):
        tok[p, me] = tok_out_buf[p * ROWS : (p + 1) * ROWS, :]
    loads[1].wait()

    half = LANES // 2
    hb = had.shape[0]
    ha = units // hb
    corner[...] = jnp.zeros_like(corner)
    corner[:hb, :hb] = had[...].astype(jnp.float32)
    left_bits = lax.broadcasted_iota(jnp.int32, (ha, ha), 0) & lax.broadcasted_iota(jnp.int32, (ha, ha), 1)
    parity = jnp.zeros((ha, ha), jnp.int32)
    for level in range(ha.bit_length() - 1):
        parity = parity ^ (jnp.right_shift(left_bits, level) & 1)
    corner[half : half + ha, half : half + ha] = (1 - 2 * parity).astype(jnp.float32)

    def digits(unit):
        high = jnp.floor((unit + 0.5) * (1.0 / hb))
        return high, unit - hb * high

    def wide(i, carry):
        shape = (LANES, LANES)
        unit = (lax.broadcasted_iota(jnp.int32, shape, 1) + i * LANES).astype(jnp.float32)
        at = lax.broadcasted_iota(jnp.int32, shape, 0).astype(jnp.float32)
        high, low = digits(unit)
        pick = jnp.where((at == low) | (at == high + half), 1.0, 0.0).astype(jnp.bfloat16)
        table[i] = jnp.dot(
            corner[...].astype(jnp.bfloat16), pick, preferred_element_type=jnp.float32
        ).astype(jnp.bfloat16)
        return carry

    lax.fori_loop(0, owners, wide, 0)
    factors = jnp.concatenate([table[j] for j in range(owners)], axis=1)

    def build(i, carry):
        shape = (LANES, LANES)
        unit = (lax.broadcasted_iota(jnp.int32, shape, 0) + i * LANES).astype(jnp.float32)
        at = lax.broadcasted_iota(jnp.int32, shape, 1).astype(jnp.float32)
        high, low = digits(unit)
        pick = jnp.concatenate(
            [jnp.where(at == low, 1.0, 0.0), jnp.where(at == high + half, 1.0, 0.0)], axis=0
        ).astype(jnp.bfloat16)
        both = jnp.dot(pick, factors, preferred_element_type=jnp.float32)
        rows = pl.ds(pl.multiple_of(i * LANES, LANES), LANES)
        local[rows, :] = (both[:LANES] * both[LANES:]).astype(jnp.bfloat16)
        return carry

    lax.fori_loop(0, owners // 2, build, 0)

    pl.semaphore_wait(barrier, n - 1)

    def remote(src, dst, send_sem, recv_sem, peer):
        return pltpu.make_async_remote_copy(
            src_ref=src, dst_ref=dst, send_sem=send_sem, recv_sem=recv_sem,
            device_id={"hx": peer}, device_id_type=pl.DeviceIdType.MESH,
        )

    def tok_out(p, i):
        return remote(
            tok_out_buf.at[pl.ds(p * ROWS, ROWS)], tok.at[p, me], tok_send.at[p, i], tok_recv.at[p, me], peers[i]
        )

    def tok_in(p, i):
        return remote(
            tok_out_buf.at[pl.ds(p * ROWS, ROWS)], tok.at[p, peers[i]], tok_send.at[p, i], tok_recv.at[p, peers[i]],
            peers[i],
        )

    for p in range(pieces):
        for i in range(n - 1):
            tok_out(p, i).start()

    lhs[...] = jnp.zeros_like(lhs)
    acc[...] = jnp.zeros_like(acc)
    lax.fori_loop(owners // 2, owners, build, 0)
    for copy in loads[2:]:
        copy.wait()

    pairs_piece = ROWS // 2
    chunks_piece = chunks // pieces
    pairs_chunk = CHUNK_GROUPS // 2
    for p in range(pieces):
        for i in range(n - 1):
            tok_in(p, i).wait_recv()
        stage[...] = tok[p].reshape(n * ROWS, LANES).astype(jnp.float32)
        for q in range(pairs_piece):
            lhs[q, :n, :LANES] = stage[pl.ds(2 * q, n, stride=ROWS), :].astype(jnp.bfloat16)
            lhs[q, n:, LANES:] = stage[pl.ds(2 * q + 1, n, stride=ROWS), :].astype(jnp.bfloat16)

        def step(k, carry):
            c = p * chunks_piece + k
            slot = lax.rem(c, SLOTS)
            gate_copy(c, slot).wait()
            up_copy(c, slot).wait()
            for q in range(pairs_chunk):
                left = lhs[k * pairs_chunk + q]
                row = c * CHUNK_GROUPS + 2 * q
                for w, scale in ((0, gs), (1, us)):
                    res = jnp.dot(
                        left, ring[slot, w, 2 * q * LANES : 2 * (q + 1) * LANES, :],
                        preferred_element_type=jnp.float32,
                    )
                    acc[w] += res[:n] * scale[pl.ds(row, 1), :] + res[n:] * scale[pl.ds(row + 1, 1), :]

            @pl.when(c + SLOTS < chunks)
            def _():
                gate_copy(c + SLOTS, slot).start()
                up_copy(c + SLOTS, slot).start()

            @pl.when(jnp.logical_and(c + SLOTS >= chunks, c + SLOTS - chunks < down_chunks))
            def _():
                down_copy(c + SLOTS - chunks).start()

            return carry

        lax.fori_loop(0, chunks_piece, step, 0)
    for c in range(SLOTS, down_chunks):
        down_copy(c).start()

    gate = acc[0]
    hidden = (gate / (1.0 + jnp.exp(-gate)) * acc[1]).astype(jnp.bfloat16)
    turned = jnp.dot(hidden, local[...], preferred_element_type=jnp.float32).astype(jnp.bfloat16)
    for j in range(owners):
        zbuf[j] = turned[:, j * LANES : (j + 1) * LANES]

    def z_out(j):
        return remote(zbuf.at[j], recv_z.at[me], z_send.at[j], z_recv.at[me], j)

    for j in range(owners):

        @pl.when(me != j)
        def _():
            z_out(j).start()

        @pl.when(me == j)
        def _():
            recv_z[j] = zbuf[j]

    def r_out(i):
        return remote(rbuf.at[peers[i]], rot.at[me], r_send.at[i], r_recv.at[me], peers[i])

    @pl.when(me < owners)
    def _():
        for i in range(n - 1):
            remote(zbuf.at[0], recv_z.at[peers[i]], z_send.at[0], z_recv.at[peers[i]], peers[i]).wait_recv()
        cube = [recv_z[h].astype(jnp.float32) for h in range(n)]
        span = 1
        while span < n:
            nxt = list(cube)
            for h in range(n):
                if h & span == 0:
                    nxt[h] = cube[h] + cube[h | span]
                    nxt[h | span] = cube[h] - cube[h | span]
            cube = nxt
            span *= 2
        for h in range(n):
            rbuf[h] = (cube[h] * (1.0 / math.sqrt(FF))).astype(jnp.bfloat16)
        for i in range(n - 1):
            r_out(i).start()
        rot[me] = rbuf[me]

    for j in range(owners):

        @pl.when(me != j)
        def _():
            remote(rbuf.at[0], rot.at[j], r_send.at[0], r_recv.at[j], j).wait_recv()

    rotated = jnp.concatenate([rot[j] for j in range(owners)], axis=1)

    def c_out(p, i):
        return remote(sendbuf.at[p, peers[i]], recv_c.at[p, me], c_send.at[p, i], c_recv.at[p, me], peers[i])

    def c_in(p, i):
        return remote(
            sendbuf.at[p, peers[i]], recv_c.at[p, peers[i]], c_send.at[p, i], c_recv.at[p, peers[i]], peers[i]
        )

    per_piece = down_chunks // out_pieces
    blocks = down_cols // LANES
    for p in range(out_pieces):
        for k in range(per_piece):
            c = p * per_piece + k
            down_copy(c).wait()
            res = jnp.dot(rotated, down[c], preferred_element_type=jnp.float32)
            for b in range(blocks):
                part[pl.ds(k * blocks + b, n, stride=ROWS), :] = res[:, b * LANES : (b + 1) * LANES]
        sendbuf[p] = part[...].astype(jnp.bfloat16).reshape(n, ROWS, LANES)
        for i in range(n - 1):
            c_out(p, i).start()
        recv_c[p, me] = sendbuf[p, me]

    for p in range(out_pieces):
        for i in range(n - 1):
            c_in(p, i).wait_recv()
        total = recv_c[p, 0].astype(jnp.float32)
        for h in range(1, n):
            total = total + recv_c[p, h].astype(jnp.float32)
        for r in range(ROWS):
            cols = slice((p * ROWS + r) * LANES, (p * ROWS + r + 1) * LANES)
            out_ref[:, cols] = (total[r : r + 1, :] * ds[:, cols]).astype(out_ref.dtype)

    for p in range(pieces):
        for i in range(n - 1):
            tok_out(p, i).wait_send()
    for j in range(owners):

        @pl.when(me != j)
        def _():
            z_out(j).wait_send()

    @pl.when(me < owners)
    def _():
        for i in range(n - 1):
            r_out(i).wait_send()

    for p in range(out_pieces):
        for i in range(n - 1):
            c_out(p, i).wait_send()


def fused(n, tokens, gate_codes, gate_scales, up_codes, up_scales, down_codes, down_scales, hadamard):
    depth, units = gate_codes.shape
    width = down_codes.shape[1]
    pieces = depth // (LANES * ROWS)
    out_pieces = width // (LANES * ROWS)
    owners = units // LANES
    chunk_rows = CHUNK_GROUPS * LANES
    down_cols = 8 * LANES
    bf16, f32 = jnp.bfloat16, jnp.float32
    dma = pltpu.SemaphoreType.DMA
    out = pl.pallas_call(
        functools.partial(kernel, n),
        out_shape=jax.ShapeDtypeStruct((1, width), bf16),
        in_specs=[pl.BlockSpec(memory_space=pl.ANY)] * 8,
        out_specs=pl.BlockSpec(memory_space=pltpu.VMEM),
        scratch_shapes=[
            pltpu.VMEM((SLOTS, 2, chunk_rows, units), bf16),
            pltpu.VMEM(gate_scales.shape, f32),
            pltpu.VMEM(up_scales.shape, f32),
            pltpu.VMEM((width // down_cols, units, down_cols), bf16),
            pltpu.VMEM((1, width), f32),
            pltpu.VMEM(hadamard.shape, hadamard.dtype),
            pltpu.VMEM((LANES, LANES), f32),
            pltpu.VMEM((owners, LANES, LANES), bf16),
            pltpu.VMEM((units, units), bf16),
            pltpu.VMEM((1, depth), bf16),
            pltpu.VMEM((depth // LANES, LANES), f32),
            pltpu.VMEM((depth // LANES, LANES), bf16),
            pltpu.VMEM((pieces, n, ROWS, LANES), bf16),
            pltpu.VMEM((n * ROWS, LANES), f32),
            pltpu.VMEM((ROWS // 2, 2 * n, 2 * LANES), bf16),
            pltpu.VMEM((2, n, units), f32),
            pltpu.VMEM((owners, n, LANES), bf16),
            pltpu.VMEM((n, n, LANES), bf16),
            pltpu.VMEM((n, n, LANES), bf16),
            pltpu.VMEM((owners, n, LANES), bf16),
            pltpu.VMEM((n * ROWS, LANES), f32),
            pltpu.VMEM((out_pieces, n, ROWS, LANES), bf16),
            pltpu.VMEM((out_pieces, n, ROWS, LANES), bf16),
            dma((SLOTS, 2)),
            dma((5,)),
            dma((width // down_cols,)),
            dma((pieces, n - 1)),
            dma((pieces, n)),
            dma((owners,)),
            dma((n,)),
            dma((n - 1,)),
            dma((owners,)),
            dma((out_pieces, n - 1)),
            dma((out_pieces, n)),
        ],
        compiler_params=pltpu.CompilerParams(
            collective_id=0, has_side_effects=True, vmem_limit_bytes=67043328
        ),
    )(
        tokens, gate_codes, gate_scales, up_codes, up_scales, down_codes, down_scales.reshape(1, width), hadamard,
    )
    return out


def fits(n, tokens, gate_codes, gate_scales, down_codes):
    rows, depth = tokens.shape
    units, width = down_codes.shape
    return (
        rows == 1
        and n == ROWS
        and HA % n == 0
        and HA // n <= LANES // 2
        and HB <= LANES // 2
        and depth == gate_scales.shape[0] * LANES
        and depth % (ROWS * LANES) == 0
        and width % (ROWS * LANES) == 0
        and units % LANES == 0
        and units // LANES <= n
    )


def per_device(
    tokens, gate_codes, gate_scales, up_codes, up_scales, down_codes, down_scales, hadamard
):
    n = lax.axis_size("hx")
    if fits(n, tokens, gate_codes, gate_scales, down_codes):
        return fused(
            n, tokens, gate_codes, gate_scales, up_codes, up_scales, down_codes, down_scales, hadamard
        )
    gate_weight = dequantize(gate_codes, gate_scales)
    up_weight = dequantize(up_codes, up_scales)
    tile_rows = lax.all_gather(tokens, "hx", axis=0, tiled=True)
    gate = jnp.dot(tile_rows, gate_weight, preferred_element_type=jnp.float32)
    up_part = jnp.dot(tile_rows, up_weight, preferred_element_type=jnp.float32)
    hidden = jax.nn.silu(gate) * up_part
    factor = hadamard.astype(jnp.float32)
    gathered = lax.all_to_all(
        hidden.astype(jnp.bfloat16), "hx", split_axis=0, concat_axis=1, tiled=True
    ).astype(hidden.dtype)
    row_count = gathered.shape[0]
    cube = gathered.reshape(row_count, HA, HB)
    cube = jnp.einsum("tab,ac->tcb", cube, sylvester(HA), precision=lax.Precision.HIGHEST)
    cube = jnp.einsum("tcb,bd->tcd", cube, factor, precision=lax.Precision.HIGHEST)
    turned = lax.all_to_all(
        cube.reshape(row_count, FF).astype(jnp.bfloat16),
        "hx",
        split_axis=1,
        concat_axis=0,
        tiled=True,
    ).astype(jnp.float32)
    rotated = (turned * (1.0 / math.sqrt(FF))).astype(jnp.bfloat16)
    summed = lax.psum_scatter(
        jnp.dot(rotated, down_codes, preferred_element_type=jnp.float32),
        "hx",
        scatter_dimension=0,
        tiled=True,
    )
    mixed = (summed * down_scales[None, :]).astype(jnp.bfloat16)
    return mixed


def solution(mesh):
    in_specs = (
        P(("groups", "hx"), None),
        P(None, "hx"),
        P(None, "hx"),
        P(None, "hx"),
        P(None, "hx"),
        P("hx", None),
        P(),
        P(),
    )
    out_specs = P(("groups", "hx"), None)
    return jax.shard_map(
        per_device, mesh=mesh, in_specs=in_specs, out_specs=out_specs, check_vma=False
    )
```

profile of v0, /device:TPU:0, one launch (start us, length us, event | category | flops | bytes accessed | tf_op | source)
XLA Modules:
  0.0 52.5 jit_solution(16595079276208118687)
XLA Ops:
  0.0 51.1 %shard_map.82 = bf16[1,8192]{1,0:T(2,128)(2,1)} custom-call(bf16[1,8192]{1,0:T(2,128)(2,1)} %tok_ref.1, bf16[8192,1664]{1,0:T(8,128)(2,1)} %gate_ref.1, f32[64,1664]{1,0:T(8,128)} %gscale_ref.1, bf16[8192,1664]{1,0:T(8,128)(2,1)} %up_ref.1, f32[64,1664]{1,0:T(8,128)} %uscale_ref.1, bf16[1664,8192]{1,0:T(8,128)(2,1)} %down_ref.1, f32[1,8192]{1,0:T(1,128)} %bitcast.1, ...), custom_call_target="tpu_custom_call" | custom-call | tf_op jit(solution)/shard_map/pallas_call | solution.py:316
  51.1 1.4 %copy.10 = bf16[1,8192]{1,0:T(2,128)(2,1)} copy(bf16[1,8192]{1,0:T(2,128)(2,1)} %shard_map.82) | data formatting | bytes 32768
where the time goes:
time: 52.7 us; the launch traced here: 52.5 us
  Pallas kernels  51.1 us (97%)
  local copies, waits for them, and re-layouts  1.41 us (3%)
    pallas_call x1, Pallas kernels, fused(): pl.pallas_call(functools.partial(kernel, n), out_shape=jax.ShapeDtypeStru...  51.1 us
    unnamed x1, local copies, waits for them, and re-layouts  1.41 us

commit v1 on v0

v1 whole, which is shorter than its diff:
```python
import functools
import math

import jax
import jax.numpy as jnp
from jax import lax
from jax.experimental import pallas as pl
from jax.experimental.pallas import tpu as pltpu
from jax.sharding import PartitionSpec as P

HA = 512
HB = 52
FF = 26624


def sylvester(size):
    index_vec = jnp.arange(size, dtype=jnp.int32)
    parity = jnp.zeros((size, size), jnp.int32)
    for level in range(max(size.bit_length() - 1, 0)):
        left_bits = jnp.right_shift(index_vec[:, None], level) & 1
        right_bits = jnp.right_shift(index_vec[None, :], level) & 1
        parity = parity + left_bits * right_bits
    return (1 - 2 * (parity % 2)).astype(jnp.float32)


def dequantize(codes, scales):
    row_total, col_total = codes.shape
    group_total = scales.shape[0]
    grouped = codes.astype(jnp.float32).reshape(group_total, row_total // group_total, col_total)
    return (grouped * scales[:, None, :]).reshape(row_total, col_total).astype(jnp.bfloat16)


LANES = 128
WIDE = 2 * LANES
PIECES = 4
CHUNK = 512
SLOTS = 6
DOWN_COLS = 1024
DOWN_SLOTS = 3
BLOCK = 64
OUT_ROWS = 16


def kernel(
    n, groups, tok_ref, gate_ref, gscale_ref, up_ref, uscale_ref, down_ref, dscale_ref, had_ref,
    out_ref,
    ring, weights, dring, down, gs, us, ds, had, corner, table, local, tok_row, tok_f32, tok_out, tok, stage, lhs, acc,
    xsend, xrecv, zbuf, recv_z, rbuf, rot, part, pair_out, pair_in, sums, recv_c,
    ring_sem, load_sem, down_sem, tok_ssem, tok_rsem, fwd_ssem, fwd_rsem, x_ssem, x_rsem, z_ssem, z_rsem, r_ssem, r_rsem,
    p_ssem, p_rsem, c_ssem, c_rsem,
):
    f32, bf16, f8 = jnp.float32, jnp.bfloat16, jnp.float8_e4m3fn
    mine = lax.axis_index("groups")
    me = lax.axis_index("hx")
    chips = n // 2
    chip, core = lax.div(me, 2), lax.rem(me, 2)
    units = gate_ref.shape[1]
    tiles = units // LANES
    half_rows = gate_ref.shape[0] // groups
    chunks = half_rows // CHUNK
    piece_rows = tok.shape[3]
    down_chunks = down.shape[0]
    other = lax.rem(mine + 1, groups)

    def device(group, index):
        return {"groups": group, "hx": index}

    def remote(src, dst, send_sem, recv_sem, peer):
        return pltpu.make_async_remote_copy(
            src_ref=src, dst_ref=dst, send_sem=send_sem, recv_sem=recv_sem,
            device_id=peer, device_id_type=pl.DeviceIdType.MESH,
        )

    def chip_at(step):
        return lax.rem(chip + step, chips)

    partner = device(mine, chip * 2 + 1 - core)
    peers = [device(mine, lax.rem(me + step, n)) for step in range(1, n)]
    across = [device(other, chip_at(step) * 2 + core) for step in range(chips)]

    def weight_copies(c):
        rows = pl.ds(pl.multiple_of(mine * half_rows + c * CHUNK, CHUNK), CHUNK)
        slot = c % SLOTS
        return [
            pltpu.make_async_copy(src.at[rows], ring.at[slot, w], ring_sem.at[slot, w])
            for w, src in enumerate((gate_ref, up_ref))
        ]

    def down_copy(c):
        cols = pl.ds(c * DOWN_COLS, DOWN_COLS)
        return pltpu.make_async_copy(down_ref.at[:, cols], dring.at[c % DOWN_SLOTS], down_sem.at[c % DOWN_SLOTS])

    scale_rows = gs.shape[0]
    half_scales = pl.ds(pl.multiple_of(mine * scale_rows, scale_rows), scale_rows)
    loads = [
        pltpu.make_async_copy(src, dst, load_sem.at[i])
        for i, (src, dst) in enumerate(
            (
                (tok_ref, tok_row), (had_ref, had), (dscale_ref, ds),
                (gscale_ref.at[half_scales], gs), (uscale_ref.at[half_scales], us),
            )
        )
    ]

    barrier = pltpu.get_barrier_semaphore()
    for peer in peers + across:
        pl.semaphore_signal(barrier, inc=1, device_id=peer, device_id_type=pl.DeviceIdType.MESH)
    for copy in loads:
        copy.start()
    for c in range(SLOTS):
        for copy in weight_copies(c):
            copy.start()
    loads[0].wait()
    row = tok_row[...].astype(f32)
    for k in range(tok_f32.shape[0]):
        tok_f32[k : k + 1, :] = row[:, k * LANES : (k + 1) * LANES]
    for h in range(groups):
        for p in range(PIECES):
            start = (h * PIECES + p) * piece_rows
            tok_out[h, p] = tok_f32[start : start + piece_rows, :].astype(bf16)
    for p in range(PIECES):
        tok[p, core, chip] = tok_out[mine, p]
    loads[1].wait()

    half = LANES // 2
    hb = had.shape[0]
    ha = units // hb
    corner[...] = jnp.zeros_like(corner)
    corner[:hb, :hb] = had[...].astype(f32)
    left_bits = lax.broadcasted_iota(jnp.int32, (ha, ha), 0) & lax.broadcasted_iota(jnp.int32, (ha, ha), 1)
    parity = jnp.zeros((ha, ha), jnp.int32)
    for level in range(ha.bit_length() - 1):
        parity = parity ^ (jnp.right_shift(left_bits, level) & 1)
    corner[half : half + ha, half : half + ha] = (1 - 2 * parity).astype(f32)

    def digits(unit):
        high = jnp.floor((unit + 0.5) * (1.0 / hb))
        return high, unit - hb * high

    def wide(i, carry):
        shape = (LANES, LANES)
        unit = (lax.broadcasted_iota(jnp.int32, shape, 1) + i * LANES).astype(f32)
        at = lax.broadcasted_iota(jnp.int32, shape, 0).astype(f32)
        high, low = digits(unit)
        pick = jnp.where((at == low) | (at == high + half), 1.0, 0.0).astype(bf16)
        table[i] = jnp.dot(corner[...].astype(bf16), pick, preferred_element_type=f32).astype(bf16)
        return carry

    lax.fori_loop(0, tiles, wide, 0)
    factors = jnp.concatenate([table[j] for j in range(tiles)], axis=1)

    def build(i, carry):
        shape = (LANES, LANES)
        unit = (lax.broadcasted_iota(jnp.int32, shape, 0) + i * LANES).astype(f32)
        at = lax.broadcasted_iota(jnp.int32, shape, 1).astype(f32)
        high, low = digits(unit)
        pick = jnp.concatenate(
            [jnp.where(at == low, 1.0, 0.0), jnp.where(at == high + half, 1.0, 0.0)], axis=0
        ).astype(bf16)
        both = jnp.dot(pick, factors, preferred_element_type=f32)
        rows = pl.ds(pl.multiple_of(i * LANES, LANES), LANES)
        local[rows, :] = (both[:LANES] * both[LANES:]).astype(f8)
        return carry

    lax.fori_loop(0, tiles // 2, build, 0)

    pl.semaphore_wait(barrier, len(peers) + len(across))

    hops = [(d, step) for d in range(groups) for step in range(chips) if (d, step) != (0, 0)]

    def tok_send(p, d, step):
        group = lax.rem(mine + d, groups)
        return remote(
            tok_out.at[group, p], tok.at[p, core, d * chips + chip], tok_ssem.at[p, d * chips + step],
            tok_rsem.at[p, d * chips + chip], device(group, chip_at(step) * 2 + core),
        )

    def tok_arrive(p, d, step):
        source = d * chips + chip_at(step)
        return remote(
            tok_out.at[0, p], tok.at[p, core, source], tok_ssem.at[p, d * chips + step], tok_rsem.at[p, source],
            device(lax.rem(mine + d, groups), chip_at(step) * 2 + core),
        )

    def forward(p, which):
        return remote(tok.at[p, which], tok.at[p, which], fwd_ssem.at[p], fwd_rsem.at[p], partner)

    for p in range(PIECES):
        for d, step in hops:
            tok_send(p, d, step).start()

    lhs[...] = jnp.zeros_like(lhs)
    acc[...] = jnp.zeros_like(acc)
    lax.fori_loop(tiles // 2, tiles, build, 0)

    def convert(c):
        for copy in weight_copies(c):
            copy.wait()

        def block(k, carry):
            rows = pl.ds(pl.multiple_of(k * BLOCK, BLOCK), BLOCK)
            to = pl.ds(pl.multiple_of(c * CHUNK + k * BLOCK, BLOCK), BLOCK)
            for w in range(2):
                weights[w, to, :] = ring[c % SLOTS, w, rows, :].astype(f8)
            return carry

        lax.fori_loop(0, CHUNK // BLOCK, block, 0)
        if c + SLOTS < chunks:
            for copy in weight_copies(c + SLOTS):
                copy.start()
        elif c + SLOTS - chunks < DOWN_SLOTS:
            down_copy(c + SLOTS - chunks).start()

    def convert_down(c):
        down_copy(c).wait()

        def block(k, carry):
            rows = pl.ds(pl.multiple_of(k * BLOCK, BLOCK), BLOCK)
            down[c, rows, :] = dring[c % DOWN_SLOTS, rows, :].astype(f8)
            return carry

        lax.fori_loop(0, units // BLOCK, block, 0)
        if c + DOWN_SLOTS < down_chunks:
            down_copy(c + DOWN_SLOTS).start()

    def relay(p):
        for d, step in hops:
            tok_arrive(p, d, step).wait_recv()
        forward(p, core).start()

    def ready(p):
        forward(p, 1 - core).wait_recv()
        stage[...] = tok[p].reshape(stage.shape).astype(f32)
        for k in range(piece_rows):
            part_rows = [
                stage[pl.ds(w * n * piece_rows + k, n, stride=piece_rows), :] for w in range(2)
            ]
            both = jnp.concatenate(
                [part_rows[0][:chips], part_rows[1][:chips], part_rows[0][chips:], part_rows[1][chips:]], axis=0
            ).astype(bf16)
            q, odd = divmod(k, 2)
            lhs[q, odd * 2 * n : (odd + 1) * 2 * n, odd * LANES : (odd + 1) * LANES] = both

    def products(p, cols, tail):
        sums_now = [None, None]
        for q in range(piece_rows // 2):
            left = lhs[q]
            row = p * piece_rows + 2 * q
            rows = slice(row * LANES, (row + 2) * LANES)
            if tail:
                right = jnp.concatenate([weights[0, rows, cols], weights[1, rows, cols]], axis=1)
                scale = jnp.concatenate([gs[row : row + 2, cols], us[row : row + 2, cols]], axis=1)
                sides = [(right, scale)]
            else:
                sides = [(weights[w, rows, cols], scale[row : row + 2, cols]) for w, scale in ((0, gs), (1, us))]
            for w, (right, scale) in enumerate(sides):
                res = jnp.dot(left, right, preferred_element_type=f32)
                new = res[: 2 * n] * scale[0:1, :] + res[2 * n :] * scale[1:2, :]
                sums_now[w] = new if sums_now[w] is None else sums_now[w] + new
        if tail:
            width = sums_now[0].shape[1] // 2
            return sums_now[0][:, :width], sums_now[0][:, width:]
        return sums_now

    spans = [(at, min(WIDE, units - at)) for at in range(0, units, WIDE)]

    def x_send(j, width):
        at = (j, slice(None), slice(None), pl.ds(0, width))
        return remote(xsend.at[at], xrecv.at[at], x_ssem.at[j], x_rsem.at[j], across[0])

    def run(p):
        for j, (at, width) in enumerate(spans):
            cols = slice(at, at + width)
            pair = products(p, cols, width < WIDE)
            for w in range(2):
                if p + 1 < PIECES:
                    acc[w, :, cols] += pair[w]
                else:
                    total = acc[w, :, cols] + pair[w]
                    acc[w, :n, cols] = total[:n]
                    xsend[j, w, :, :width] = total[n:].astype(bf16)
            if p + 1 == PIECES:
                x_send(j, width).start()

    for copy in loads[2:]:
        copy.wait()
    early = chunks - 2
    for c in range(early):
        convert(c)
    relay(0)
    convert(early)
    relay(1)
    convert(early + 1)
    for p in range(PIECES):
        ready(p)
        run(p)
        if p + 2 < PIECES:
            relay(p + 2)

    for c in range(2):
        convert_down(c)
    turned = None
    for j, (at, width) in enumerate(spans):
        x_send(j, width).wait_recv()
        cols = slice(at, at + width)
        gate = acc[0, :n, cols] + xrecv[j, 0, :, :width].astype(f32)
        lift = acc[1, :n, cols] + xrecv[j, 1, :, :width].astype(f32)
        hidden = (gate / (1.0 + jnp.exp(-gate)) * lift).astype(bf16)
        new = jnp.dot(hidden, local[cols, :], preferred_element_type=f32)
        turned = new if turned is None else turned + new
    turned = turned.astype(bf16)

    owners = zbuf.shape[0]
    quarter = n // 4

    def owner_at(o):
        return quarter + (o % 2) * quarter + o // 2

    def held(o):
        return len(range(o, tiles, owners))

    for j in range(tiles):
        zbuf[j % owners, j // owners] = turned[:, j * LANES : (j + 1) * LANES]

    def z_out(o):
        count = pl.ds(0, held(o))
        return remote(
            zbuf.at[o, count], recv_z.at[me, count], z_ssem.at[o], z_rsem.at[me], device(mine, owner_at(o))
        )

    for o in range(owners):

        @pl.when(me != owner_at(o))
        def _():
            z_out(o).start()

        @pl.when(me == owner_at(o))
        def _():
            recv_z[me] = zbuf[o]

    for c in range(2, 5):
        convert_down(c)

    place = me - quarter
    number = lax.rem(place, quarter) * 2 + lax.div(place, quarter)
    owns = jnp.logical_and(me >= quarter, me < 3 * quarter)
    extra = tiles % owners
    scale = 1.0 / math.sqrt(units * n)

    def r_out(i, count):
        at = pl.ds(0, count)
        peer = lax.rem(me + i, n)
        return remote(rbuf.at[peer, at], rot.at[number, at], r_ssem.at[i - 1], r_rsem.at[number], device(mine, peer))

    def turn(count):
        at = pl.ds(0, count)
        for i in range(1, n):
            peer = lax.rem(me + i, n)
            remote(
                zbuf.at[0, at], recv_z.at[peer, at], z_ssem.at[0], z_rsem.at[peer], device(mine, peer)
            ).wait_recv()
        for t in range(count):
            cube = [recv_z[h, t].astype(f32) for h in range(n)]
            span = 1
            while span < n:
                nxt = list(cube)
                for h in range(n):
                    if h & span == 0:
                        nxt[h] = cube[h] + cube[h | span]
                        nxt[h | span] = cube[h] - cube[h | span]
                cube = nxt
                span *= 2
            for h in range(n):
                rbuf[h, t] = (cube[h] * scale).astype(bf16)
        for i in range(1, n):
            r_out(i, count).start()
        rot[number] = rbuf[me]

    many, few = held(0), held(owners - 1)

    def by_count(action):
        if extra == 0:
            pl.when(owns)(lambda: action(many))
        else:
            pl.when(jnp.logical_and(owns, number < extra))(lambda: action(many))
            pl.when(jnp.logical_and(owns, number >= extra))(lambda: action(few))

    by_count(turn)

    for c in range(5, down_chunks):
        convert_down(c)

    for o in range(owners):

        @pl.when(me != owner_at(o))
        def _():
            count = pl.ds(0, held(o))
            remote(
                rbuf.at[0, count], rot.at[o, count], r_ssem.at[0], r_rsem.at[o], device(mine, owner_at(o))
            ).wait_recv()

    rotated = jnp.concatenate([rot[j % owners, j // owners] for j in range(tiles)], axis=1)

    out_pieces = recv_c.shape[0]
    per_piece = down_chunks // out_pieces
    blocks = DOWN_COLS // LANES
    own_rows = chips * OUT_ROWS

    def pair_copy(p, which):
        at = pl.ds(which * chips, chips)
        return remote(pair_out.at[p, at], pair_in.at[p], p_ssem.at[p], p_rsem.at[p], partner)

    def c_out(p, step):
        to = chip_at(step)
        return remote(
            sums.at[p, to], recv_c.at[p, chip], c_ssem.at[p, step - 1], c_rsem.at[p, chip], device(mine, to * 2 + core)
        )

    def c_in(p, step):
        source = chip_at(step)
        return remote(
            sums.at[p, source], recv_c.at[p, source], c_ssem.at[p, step - 1], c_rsem.at[p, source],
            device(mine, source * 2 + core),
        )

    def finish(p):
        pair_copy(p, core).wait_recv()
        rows = pl.ds(pl.multiple_of(core * own_rows, own_rows), own_rows)
        both = part[p, rows, :] + pair_in[p].reshape(own_rows, LANES).astype(f32)
        sums[p] = both.astype(bf16).reshape(chips, OUT_ROWS, LANES)
        for step in range(1, chips):
            c_out(p, step).start()
        recv_c[p, chip] = sums[p, chip]

    for p in range(out_pieces):
        for k in range(per_piece):
            res = jnp.dot(rotated, down[p * per_piece + k], preferred_element_type=f32)
            for b in range(blocks):
                part[p, pl.ds(k * blocks + b, n, stride=OUT_ROWS), :] = res[:, b * LANES : (b + 1) * LANES]
        pair_out[p] = part[p].astype(bf16).reshape(n, OUT_ROWS, LANES)
        pair_copy(p, 1 - core).start()
        if p > 0:
            finish(p - 1)
    finish(out_pieces - 1)

    for p in range(out_pieces):
        for step in range(1, chips):
            c_in(p, step).wait_recv()
        total = recv_c[p, 0].astype(f32)
        for h in range(1, chips):
            total = total + recv_c[p, h].astype(f32)
        for r in range(OUT_ROWS):
            cols = slice((p * OUT_ROWS + r) * LANES, (p * OUT_ROWS + r + 1) * LANES)
            out_ref[:, cols] = (total[r : r + 1, :] * ds[:, cols]).astype(out_ref.dtype)

    for p in range(PIECES):
        for d, step in hops:
            tok_send(p, d, step).wait_send()
        forward(p, core).wait_send()
    for j, (at, width) in enumerate(spans):
        x_send(j, width).wait_send()
    for o in range(owners):

        @pl.when(me != owner_at(o))
        def _():
            z_out(o).wait_send()

    def drain(count):
        for i in range(1, n):
            r_out(i, count).wait_send()

    by_count(drain)
    for p in range(out_pieces):
        pair_copy(p, 1 - core).wait_send()
        for step in range(1, chips):
            c_out(p, step).wait_send()


def fused(n, groups, tokens, gate_codes, gate_scales, up_codes, up_scales, down_codes, down_scales, hadamard):
    depth, units = gate_codes.shape
    width = down_codes.shape[1]
    tiles = units // LANES
    piece_rows = depth // (groups * PIECES * LANES)
    half_scales = (gate_scales.shape[0] // groups, units)
    out_pieces = width // (LANES * OUT_ROWS)
    owners = n // 2
    held = -(-tiles // owners)
    spans = -(-units // WIDE)
    chips = n // 2
    bf16, f32, f8 = jnp.bfloat16, jnp.float32, jnp.float8_e4m3fn
    dma = pltpu.SemaphoreType.DMA
    vmem = pltpu.VMEM
    return pl.pallas_call(
        functools.partial(kernel, n, groups),
        out_shape=jax.ShapeDtypeStruct((1, width), bf16),
        in_specs=[pl.BlockSpec(memory_space=pl.ANY)] * 8,
        out_specs=pl.BlockSpec(memory_space=pltpu.VMEM),
        scratch_shapes=[
            vmem((SLOTS, 2, CHUNK, units), bf16),
            vmem((2, depth // groups, units), f8),
            vmem((DOWN_SLOTS, units, DOWN_COLS), bf16),
            vmem((width // DOWN_COLS, units, DOWN_COLS), f8),
            vmem(half_scales, f32),
            vmem(half_scales, f32),
            vmem((1, width), f32),
            vmem(hadamard.shape, hadamard.dtype),
            vmem((LANES, LANES), f32),
            vmem((tiles, LANES, LANES), bf16),
            vmem((units, units), f8),
            vmem((1, depth), bf16),
            vmem((depth // LANES, LANES), f32),
            vmem((groups, PIECES, piece_rows, LANES), bf16),
            vmem((PIECES, 2, n, piece_rows, LANES), bf16),
            vmem((2 * n * piece_rows, LANES), f32),
            vmem((piece_rows // 2, 4 * n, WIDE), bf16),
            vmem((2, 2 * n, units), f32),
            vmem((spans, 2, n, WIDE), bf16),
            vmem((spans, 2, n, WIDE), bf16),
            vmem((owners, held, n, LANES), bf16),
            vmem((n, held, n, LANES), bf16),
            vmem((n, held, n, LANES), bf16),
            vmem((owners, held, n, LANES), bf16),
            vmem((out_pieces, n * OUT_ROWS, LANES), f32),
            vmem((out_pieces, n, OUT_ROWS, LANES), bf16),
            vmem((out_pieces, chips, OUT_ROWS, LANES), bf16),
            vmem((out_pieces, chips, OUT_ROWS, LANES), bf16),
            vmem((out_pieces, chips, OUT_ROWS, LANES), bf16),
            dma((SLOTS, 2)),
            dma((5,)),
            dma((DOWN_SLOTS,)),
            dma((PIECES, n)),
            dma((PIECES, n)),
            dma((PIECES,)),
            dma((PIECES,)),
            dma((spans,)),
            dma((spans,)),
            dma((owners,)),
            dma((n,)),
            dma((n - 1,)),
            dma((owners,)),
            dma((out_pieces,)),
            dma((out_pieces,)),
            dma((out_pieces, chips - 1)),
            dma((out_pieces, chips)),
        ],
        compiler_params=pltpu.CompilerParams(
            collective_id=0, has_side_effects=True, vmem_limit_bytes=67043328
        ),
    )(
        tokens, gate_codes, gate_scales, up_codes, up_scales, down_codes, down_scales.reshape(1, width), hadamard,
    )


def fits(n, groups, tokens, gate_scales, down_codes):
    rows, depth = tokens.shape
    units, width = down_codes.shape
    scale_rows = gate_scales.shape[0]
    return (
        rows == 1
        and n == 16
        and groups == 2
        and HA % n == 0
        and units * n == HA * HB
        and HA // n <= LANES // 2
        and HB <= LANES // 2
        and depth == scale_rows * LANES
        and scale_rows % (groups * PIECES * 8) == 0
        and depth == 8 * groups * CHUNK
        and width == 8 * DOWN_COLS
        and units % LANES == 0
        and n // 2 <= units // LANES <= n
    )


def per_device(
    tokens, gate_codes, gate_scales, up_codes, up_scales, down_codes, down_scales, hadamard
):
    n = lax.axis_size("hx")
    groups = lax.axis_size("groups")
    if fits(n, groups, tokens, gate_scales, down_codes):
        return fused(
            n, groups, tokens, gate_codes, gate_scales, up_codes, up_scales, down_codes, down_scales, hadamard
        )
    gate_weight = dequantize(gate_codes, gate_scales)
    up_weight = dequantize(up_codes, up_scales)
    tile_rows = lax.all_gather(tokens, "hx", axis=0, tiled=True)
    gate = jnp.dot(tile_rows, gate_weight, preferred_element_type=jnp.float32)
    up_part = jnp.dot(tile_rows, up_weight, preferred_element_type=jnp.float32)
    hidden = jax.nn.silu(gate) * up_part
    factor = hadamard.astype(jnp.float32)
    gathered = lax.all_to_all(
        hidden.astype(jnp.bfloat16), "hx", split_axis=0, concat_axis=1, tiled=True
    ).astype(hidden.dtype)
    row_count = gathered.shape[0]
    cube = gathered.reshape(row_count, HA, HB)
    cube = jnp.einsum("tab,ac->tcb", cube, sylvester(HA), precision=lax.Precision.HIGHEST)
    cube = jnp.einsum("tcb,bd->tcd", cube, factor, precision=lax.Precision.HIGHEST)
    turned = lax.all_to_all(
        cube.reshape(row_count, FF).astype(jnp.bfloat16),
        "hx",
        split_axis=1,
        concat_axis=0,
        tiled=True,
    ).astype(jnp.float32)
    rotated = (turned * (1.0 / math.sqrt(FF))).astype(jnp.bfloat16)
    summed = lax.psum_scatter(
        jnp.dot(rotated, down_codes, preferred_element_type=jnp.float32),
        "hx",
        scatter_dimension=0,
        tiled=True,
    )
    mixed = (summed * down_scales[None, :]).astype(jnp.bfloat16)
    return mixed


def solution(mesh):
    in_specs = (
        P(("groups", "hx"), None),
        P(None, "hx"),
        P(None, "hx"),
        P(None, "hx"),
        P(None, "hx"),
        P("hx", None),
        P(),
        P(),
    )
    out_specs = P(("groups", "hx"), None)
    return jax.shard_map(
        per_device, mesh=mesh, in_specs=in_specs, out_specs=out_specs, check_vma=False
    )
```

time: 52.7 us -> 47.7 us (0.905)
  Pallas kernels: 51.1 us -> 46.1 us
    pallas_call x1, Pallas kernels: 51.1 us -> 46.1 us  [fused(): pl.pallas_call(functools.partial(kernel, n, groups), out_shape=jax.ShapeD...]
where the time goes in v1:
time: 47.7 us; the launch traced here: 47.5 us
  Pallas kernels  46.1 us (97%)
  local copies, waits for them, and re-layouts  1.41 us (3%)
    pallas_call x1, Pallas kernels, fused(): pl.pallas_call(functools.partial(kernel, n, groups), out_shape=jax.ShapeD...  46.1 us
    unnamed x1, local copies, waits for them, and re-layouts  1.41 us

profile of v1, /device:TPU:0, one launch (start us, length us, event | category | flops | bytes accessed | tf_op | source)
XLA Modules:
  0.0 47.5 jit_solution(724301589325562328)
XLA Ops:
  0.0 46.1 %shard_map.82 = bf16[1,8192]{1,0:T(2,128)(2,1)} custom-call(bf16[1,8192]{1,0:T(2,128)(2,1)} %tok_ref.1, bf16[8192,1664]{1,0:T(8,128)(2,1)} %gate_ref.1, f32[64,1664]{1,0:T(8,128)} %gscale_ref.1, bf16[8192,1664]{1,0:T(8,128)(2,1)} %up_ref.1, f32[64,1664]{1,0:T(8,128)} %uscale_ref.1, bf16[1664,8192]{1,0:T(8,128)(2,1)} %down_ref.1, f32[1,8192]{1,0:T(1,128)} %bitcast.1, ...), custom_call_target="tpu_custom_call" | custom-call | tf_op jit(solution)/shard_map/pallas_call | solution.py:493
  46.1 1.4 %copy.10 = bf16[1,8192]{1,0:T(2,128)(2,1)} copy(bf16[1,8192]{1,0:T(2,128)(2,1)} %shard_map.82) | data formatting | bytes 32768

commit v2 on v1

--- a/solution.py
+++ b/solution.py
@@ -78,13 +78,13 @@
     peers = [device(mine, lax.rem(me + step, n)) for step in range(1, n)]
     across = [device(other, chip_at(step) * 2 + core) for step in range(chips)]
 
-    def weight_copies(c):
+    def start_weights(c, slot):
         rows = pl.ds(pl.multiple_of(mine * half_rows + c * CHUNK, CHUNK), CHUNK)
-        slot = c % SLOTS
-        return [
-            pltpu.make_async_copy(src.at[rows], ring.at[slot, w], ring_sem.at[slot, w])
-            for w, src in enumerate((gate_ref, up_ref))
-        ]
+        for w, src in enumerate((gate_ref, up_ref)):
+            pltpu.make_async_copy(src.at[rows], ring.at[slot, w], ring_sem.at[slot]).start()
+
+    def wait_weights(slot):
+        pltpu.make_async_copy(ring.at[slot], ring.at[slot], ring_sem.at[slot]).wait()
 
     def down_copy(c):
         cols = pl.ds(c * DOWN_COLS, DOWN_COLS)
@@ -107,9 +107,12 @@
         pl.semaphore_signal(barrier, inc=1, device_id=peer, device_id_type=pl.DeviceIdType.MESH)
     for copy in loads:
         copy.start()
-    for c in range(SLOTS):
-        for copy in weight_copies(c):
-            copy.start()
+
+    def first(c, carry):
+        start_weights(c, c)
+        return carry
+
+    lax.fori_loop(0, SLOTS, first, 0)
     loads[0].wait()
     row = tok_row[...].astype(f32)
     for k in range(tok_f32.shape[0]):
@@ -137,17 +140,14 @@
         high = jnp.floor((unit + 0.5) * (1.0 / hb))
         return high, unit - hb * high
 
-    def wide(i, carry):
-        shape = (LANES, LANES)
-        unit = (lax.broadcasted_iota(jnp.int32, shape, 1) + i * LANES).astype(f32)
-        at = lax.broadcasted_iota(jnp.int32, shape, 0).astype(f32)
-        high, low = digits(unit)
+    at = lax.broadcasted_iota(jnp.int32, (LANES, LANES), 0).astype(f32)
+    unit = lax.broadcasted_iota(jnp.int32, (LANES, LANES), 1).astype(f32)
+    parts = corner[...].astype(bf16)
+    for i in range(tiles):
+        high, low = digits(unit + float(i * LANES))
         pick = jnp.where((at == low) | (at == high + half), 1.0, 0.0).astype(bf16)
-        table[i] = jnp.dot(corner[...].astype(bf16), pick, preferred_element_type=f32).astype(bf16)
-        return carry
-
-    lax.fori_loop(0, tiles, wide, 0)
-    factors = jnp.concatenate([table[j] for j in range(tiles)], axis=1)
+        table[:, i * LANES : (i + 1) * LANES] = jnp.dot(parts, pick, preferred_element_type=f32).astype(bf16)
+    factors = table[...]
 
     def build(i, carry):
         shape = (LANES, LANES)
@@ -162,7 +162,16 @@
         local[rows, :] = (both[:LANES] * both[LANES:]).astype(f8)
         return carry
 
-    lax.fori_loop(0, tiles // 2, build, 0)
+    octet = 8 * hb
+    lax.fori_loop(0, -(-octet // LANES), build, 0)
+
+    def signs(k, carry):
+        rows = pl.ds(pl.multiple_of(k * 32, 32), 32)
+        base = local[rows, :].astype(bf16)
+        for i in range(1, ha // 8):
+            to = pl.ds(pl.multiple_of(i * octet + k * 32, 32), 32)
+            local[to, :] = (base * table[half + 8 * i : half + 8 * i + 1, :]).astype(f8)
+        return carry
 
     pl.semaphore_wait(barrier, len(peers) + len(across))
 
@@ -171,16 +180,14 @@
     def tok_send(p, d, step):
         group = lax.rem(mine + d, groups)
         return remote(
-            tok_out.at[group, p], tok.at[p, core, d * chips + chip], tok_ssem.at[p, d * chips + step],
-            tok_rsem.at[p, d * chips + chip], device(group, chip_at(step) * 2 + core),
+            tok_out.at[group, p], tok.at[p, core, d * chips + chip], tok_ssem.at[p], tok_rsem.at[p],
+            device(group, chip_at(step) * 2 + core),
         )
 
-    def tok_arrive(p, d, step):
-        source = d * chips + chip_at(step)
-        return remote(
-            tok_out.at[0, p], tok.at[p, core, source], tok_ssem.at[p, d * chips + step], tok_rsem.at[p, source],
-            device(lax.rem(mine + d, groups), chip_at(step) * 2 + core),
-        )
+    def tok_all(p):
+        blocks = pl.ds(0, len(hops))
+        at = tok.at[p, core, blocks]
+        return remote(at, at, tok_ssem.at[p], tok_rsem.at[p], partner)
 
     def forward(p, which):
         return remote(tok.at[p, which], tok.at[p, which], fwd_ssem.at[p], fwd_rsem.at[p], partner)
@@ -191,11 +198,10 @@
 
     lhs[...] = jnp.zeros_like(lhs)
     acc[...] = jnp.zeros_like(acc)
-    lax.fori_loop(tiles // 2, tiles, build, 0)
+    lax.fori_loop(0, octet // 32, signs, 0)
 
     def convert(c):
-        for copy in weight_copies(c):
-            copy.wait()
+        wait_weights(c % SLOTS)
 
         def block(k, carry):
             rows = pl.ds(pl.multiple_of(k * BLOCK, BLOCK), BLOCK)
@@ -206,8 +212,7 @@
 
         lax.fori_loop(0, CHUNK // BLOCK, block, 0)
         if c + SLOTS < chunks:
-            for copy in weight_copies(c + SLOTS):
-                copy.start()
+            start_weights(c + SLOTS, c % SLOTS)
         elif c + SLOTS - chunks < DOWN_SLOTS:
             down_copy(c + SLOTS - chunks).start()
 
@@ -224,8 +229,7 @@
             down_copy(c + DOWN_SLOTS).start()
 
     def relay(p):
-        for d, step in hops:
-            tok_arrive(p, d, step).wait_recv()
+        tok_all(p).wait_recv()
         forward(p, core).start()
 
     def ready(p):
@@ -297,7 +301,7 @@
         if p + 2 < PIECES:
             relay(p + 2)
 
-    for c in range(2):
+    for c in range(3):
         convert_down(c)
     turned = None
     for j, (at, width) in enumerate(spans):
@@ -325,7 +329,7 @@
     def z_out(o):
         count = pl.ds(0, held(o))
         return remote(
-            zbuf.at[o, count], recv_z.at[me, count], z_ssem.at[o], z_rsem.at[me], device(mine, owner_at(o))
+            zbuf.at[o, count], recv_z.at[me, count], z_ssem.at[o], z_rsem.at[0], device(mine, owner_at(o))
         )
 
     for o in range(owners):
@@ -338,7 +342,7 @@
         def _():
             recv_z[me] = zbuf[o]
 
-    for c in range(2, 5):
+    for c in range(3, 6):
         convert_down(c)
 
     place = me - quarter
@@ -350,15 +354,12 @@
     def r_out(i, count):
         at = pl.ds(0, count)
         peer = lax.rem(me + i, n)
-        return remote(rbuf.at[peer, at], rot.at[number, at], r_ssem.at[i - 1], r_rsem.at[number], device(mine, peer))
+        return remote(rbuf.at[peer, at], rot.at[number, at], r_ssem.at[0], r_rsem.at[number], device(mine, peer))
 
     def turn(count):
         at = pl.ds(0, count)
-        for i in range(1, n):
-            peer = lax.rem(me + i, n)
-            remote(
-                zbuf.at[0, at], recv_z.at[peer, at], z_ssem.at[0], z_rsem.at[peer], device(mine, peer)
-            ).wait_recv()
+        every = recv_z.at[pl.ds(0, n - 1), at]
+        remote(every, every, z_ssem.at[0], z_rsem.at[0], partner).wait_recv()
         for t in range(count):
             cube = [recv_z[h, t].astype(f32) for h in range(n)]
             span = 1
@@ -387,7 +388,7 @@
 
     by_count(turn)
 
-    for c in range(5, down_chunks):
+    for c in range(6, down_chunks):
         convert_down(c)
 
     for o in range(owners):
@@ -413,15 +414,12 @@
     def c_out(p, step):
         to = chip_at(step)
         return remote(
-            sums.at[p, to], recv_c.at[p, chip], c_ssem.at[p, step - 1], c_rsem.at[p, chip], device(mine, to * 2 + core)
+            sums.at[p, to], recv_c.at[p, chip], c_ssem.at[p], c_rsem.at[p], device(mine, to * 2 + core)
         )
 
-    def c_in(p, step):
-        source = chip_at(step)
-        return remote(
-            sums.at[p, source], recv_c.at[p, source], c_ssem.at[p, step - 1], c_rsem.at[p, source],
-            device(mine, source * 2 + core),
-        )
+    def c_all(p, ref):
+        at = ref.at[p, pl.ds(0, chips - 1)]
+        return remote(at, at, c_ssem.at[p], c_rsem.at[p], partner)
 
     def finish(p):
         pair_copy(p, core).wait_recv()
@@ -444,8 +442,7 @@
     finish(out_pieces - 1)
 
     for p in range(out_pieces):
-        for step in range(1, chips):
-            c_in(p, step).wait_recv()
+        c_all(p, recv_c).wait_recv()
         total = recv_c[p, 0].astype(f32)
         for h in range(1, chips):
             total = total + recv_c[p, h].astype(f32)
@@ -454,8 +451,7 @@
             out_ref[:, cols] = (total[r : r + 1, :] * ds[:, cols]).astype(out_ref.dtype)
 
     for p in range(PIECES):
-        for d, step in hops:
-            tok_send(p, d, step).wait_send()
+        tok_all(p).wait_send()
         forward(p, core).wait_send()
     for j, (at, width) in enumerate(spans):
         x_send(j, width).wait_send()
@@ -466,14 +462,13 @@
             z_out(o).wait_send()
 
     def drain(count):
-        for i in range(1, n):
-            r_out(i, count).wait_send()
+        every = rbuf.at[pl.ds(0, n - 1), pl.ds(0, count)]
+        remote(every, every, r_ssem.at[0], r_rsem.at[0], partner).wait_send()
 
     by_count(drain)
     for p in range(out_pieces):
         pair_copy(p, 1 - core).wait_send()
-        for step in range(1, chips):
-            c_out(p, step).wait_send()
+        c_all(p, sums).wait_send()
 
 
 def fused(n, groups, tokens, gate_codes, gate_scales, up_codes, up_scales, down_codes, down_scales, hadamard):
@@ -505,7 +500,7 @@
             vmem((1, width), f32),
             vmem(hadamard.shape, hadamard.dtype),
             vmem((LANES, LANES), f32),
-            vmem((tiles, LANES, LANES), bf16),
+            vmem((LANES, units), bf16),
             vmem((units, units), f8),
             vmem((1, depth), bf16),
             vmem((depth // LANES, LANES), f32),
@@ -525,23 +520,23 @@
             vmem((out_pieces, chips, OUT_ROWS, LANES), bf16),
             vmem((out_pieces, chips, OUT_ROWS, LANES), bf16),
             vmem((out_pieces, chips, OUT_ROWS, LANES), bf16),
-            dma((SLOTS, 2)),
+            dma((SLOTS,)),
             dma((5,)),
             dma((DOWN_SLOTS,)),
-            dma((PIECES, n)),
-            dma((PIECES, n)),
+            dma((PIECES,)),
+            dma((PIECES,)),
             dma((PIECES,)),
             dma((PIECES,)),
             dma((spans,)),
             dma((spans,)),
             dma((owners,)),
-            dma((n,)),
-            dma((n - 1,)),
+            dma((1,)),
+            dma((1,)),
             dma((owners,)),
             dma((out_pieces,)),
             dma((out_pieces,)),
-            dma((out_pieces, chips - 1)),
-            dma((out_pieces, chips)),
+            dma((out_pieces,)),
+            dma((out_pieces,)),
         ],
         compiler_params=pltpu.CompilerParams(
             collective_id=0, has_side_effects=True, vmem_limit_bytes=67043328
@@ -563,6 +558,8 @@
         and units * n == HA * HB
         and HA // n <= LANES // 2
         and HB <= LANES // 2
+        and HA // n % 8 == 0
+        and 8 * HB % 32 == 0
         and depth == scale_rows * LANES
         and scale_rows % (groups * PIECES * 8) == 0
         and depth == 8 * groups * CHUNK

time: 47.7 us -> 39.3 us (0.82)
  Pallas kernels: 46.1 us -> 37.7 us
    pallas_call x1, Pallas kernels: 46.1 us -> 37.7 us  [fused(): pl.pallas_call(functools.partial(kernel, n, groups), out_shape=jax.ShapeD...]
where the time goes in v2:
time: 39.3 us; the launch traced here: 39.1 us
  Pallas kernels  37.7 us (96%)
  local copies, waits for them, and re-layouts  1.41 us (4%)
    pallas_call x1, Pallas kernels, fused(): pl.pallas_call(functools.partial(kernel, n, groups), out_shape=jax.ShapeD...  37.7 us
    unnamed x1, local copies, waits for them, and re-layouts  1.41 us

profile of v2, /device:TPU:0, one launch (start us, length us, event | category | flops | bytes accessed | tf_op | source)
XLA Modules:
  0.0 39.1 jit_solution(17759676738778003714)
XLA Ops:
  0.0 37.7 %shard_map.82 = bf16[1,8192]{1,0:T(2,128)(2,1)} custom-call(bf16[1,8192]{1,0:T(2,128)(2,1)} %tok_ref.1, bf16[8192,1664]{1,0:T(8,128)(2,1)} %gate_ref.1, f32[64,1664]{1,0:T(8,128)} %gscale_ref.1, bf16[8192,1664]{1,0:T(8,128)(2,1)} %up_ref.1, f32[64,1664]{1,0:T(8,128)} %uscale_ref.1, bf16[1664,8192]{1,0:T(8,128)(2,1)} %down_ref.1, f32[1,8192]{1,0:T(1,128)} %bitcast.1, ...), custom_call_target="tpu_custom_call" | custom-call | tf_op jit(solution)/shard_map/pallas_call | solution.py:488
  37.7 1.4 %copy.10 = bf16[1,8192]{1,0:T(2,128)(2,1)} copy(bf16[1,8192]{1,0:T(2,128)(2,1)} %shard_map.82) | data formatting | bytes 32768

commit v3 on v2

--- a/solution.py
+++ b/solution.py
@@ -32,7 +32,8 @@
 
 LANES = 128
 WIDE = 2 * LANES
-PIECES = 4
+PIECES = 2
+MERGED = 1
 CHUNK = 512
 SLOTS = 6
 DOWN_COLS = 1024
@@ -243,12 +244,12 @@
                 [part_rows[0][:chips], part_rows[1][:chips], part_rows[0][chips:], part_rows[1][chips:]], axis=0
             ).astype(bf16)
             q, odd = divmod(k, 2)
-            lhs[q, odd * 2 * n : (odd + 1) * 2 * n, odd * LANES : (odd + 1) * LANES] = both
+            lhs[p, q, odd * 2 * n : (odd + 1) * 2 * n, odd * LANES : (odd + 1) * LANES] = both
 
     def products(p, cols, tail):
         sums_now = [None, None]
         for q in range(piece_rows // 2):
-            left = lhs[q]
+            left = lhs[p, q]
             row = p * piece_rows + 2 * q
             rows = slice(row * LANES, (row + 2) * LANES)
             if tail:
@@ -272,34 +273,44 @@
         at = (j, slice(None), slice(None), pl.ds(0, width))
         return remote(xsend.at[at], xrecv.at[at], x_ssem.at[j], x_rsem.at[j], across[0])
 
-    def run(p):
+    def run(pieces):
+        final = pieces[-1] + 1 == PIECES
         for j, (at, width) in enumerate(spans):
             cols = slice(at, at + width)
-            pair = products(p, cols, width < WIDE)
+            pair = None
+            for p in pieces:
+                new = products(p, cols, width < WIDE)
+                pair = new if pair is None else [a + b for a, b in zip(pair, new)]
             for w in range(2):
-                if p + 1 < PIECES:
+                if not final:
                     acc[w, :, cols] += pair[w]
                 else:
                     total = acc[w, :, cols] + pair[w]
                     acc[w, :n, cols] = total[:n]
                     xsend[j, w, :, :width] = total[n:].astype(bf16)
-            if p + 1 == PIECES:
+            if final:
                 x_send(j, width).start()
 
     for copy in loads[2:]:
         copy.wait()
-    early = chunks - 2
+    per_piece = chunks // PIECES
+    last = PIECES - MERGED
+    early = chunks - per_piece
     for c in range(early):
         convert(c)
     relay(0)
     convert(early)
     relay(1)
-    convert(early + 1)
     for p in range(PIECES):
         ready(p)
-        run(p)
+        if p < last:
+            run([p])
         if p + 2 < PIECES:
             relay(p + 2)
+        if p == 0:
+            for c in range(early + 1, chunks):
+                convert(c)
+    run(list(range(last, PIECES)))
 
     for c in range(3):
         convert_down(c)
@@ -403,7 +414,7 @@
     rotated = jnp.concatenate([rot[j % owners, j // owners] for j in range(tiles)], axis=1)
 
     out_pieces = recv_c.shape[0]
-    per_piece = down_chunks // out_pieces
+    per_out = down_chunks // out_pieces
     blocks = DOWN_COLS // LANES
     own_rows = chips * OUT_ROWS
 
@@ -431,8 +442,8 @@
         recv_c[p, chip] = sums[p, chip]
 
     for p in range(out_pieces):
-        for k in range(per_piece):
-            res = jnp.dot(rotated, down[p * per_piece + k], preferred_element_type=f32)
+        for k in range(per_out):
+            res = jnp.dot(rotated, down[p * per_out + k], preferred_element_type=f32)
             for b in range(blocks):
                 part[p, pl.ds(k * blocks + b, n, stride=OUT_ROWS), :] = res[:, b * LANES : (b + 1) * LANES]
         pair_out[p] = part[p].astype(bf16).reshape(n, OUT_ROWS, LANES)
@@ -507,7 +518,7 @@
             vmem((groups, PIECES, piece_rows, LANES), bf16),
             vmem((PIECES, 2, n, piece_rows, LANES), bf16),
             vmem((2 * n * piece_rows, LANES), f32),
-            vmem((piece_rows // 2, 4 * n, WIDE), bf16),
+            vmem((PIECES, piece_rows // 2, 4 * n, WIDE), bf16),
             vmem((2, 2 * n, units), f32),
             vmem((spans, 2, n, WIDE), bf16),
             vmem((spans, 2, n, WIDE), bf16),

time: 39.3 us -> 37.9 us (0.964)
  Pallas kernels: 37.7 us -> 36.3 us
    pallas_call x1, Pallas kernels: 37.7 us -> 36.3 us  [fused(): pl.pallas_call(functools.partial(kernel, n, groups), out_shape=jax.ShapeD...]
where the time goes in v3:
time: 37.9 us; the launch traced here: 37.8 us
  Pallas kernels  36.3 us (96%)
  local copies, waits for them, and re-layouts  1.41 us (4%)
    pallas_call x1, Pallas kernels, fused(): pl.pallas_call(functools.partial(kernel, n, groups), out_shape=jax.ShapeD...  36.3 us
    unnamed x1, local copies, waits for them, and re-layouts  1.41 us

profile of v3, /device:TPU:0, one launch (start us, length us, event | category | flops | bytes accessed | tf_op | source)
XLA Modules:
  0.0 37.8 jit_solution(6487858604713078633)
XLA Ops:
  0.0 36.3 %shard_map.82 = bf16[1,8192]{1,0:T(2,128)(2,1)} custom-call(bf16[1,8192]{1,0:T(2,128)(2,1)} %tok_ref.1, bf16[8192,1664]{1,0:T(8,128)(2,1)} %gate_ref.1, f32[64,1664]{1,0:T(8,128)} %gscale_ref.1, bf16[8192,1664]{1,0:T(8,128)(2,1)} %up_ref.1, f32[64,1664]{1,0:T(8,128)} %uscale_ref.1, bf16[1664,8192]{1,0:T(8,128)(2,1)} %down_ref.1, f32[1,8192]{1,0:T(1,128)} %bitcast.1, ...), custom_call_target="tpu_custom_call" | custom-call | tf_op jit(solution)/shard_map/pallas_call | solution.py:499
  36.4 1.4 %copy.10 = bf16[1,8192]{1,0:T(2,128)(2,1)} copy(bf16[1,8192]{1,0:T(2,128)(2,1)} %shard_map.82) | data formatting | bytes 32768

commit v4 on v3

--- a/solution.py
+++ b/solution.py
@@ -46,7 +46,7 @@
     n, groups, tok_ref, gate_ref, gscale_ref, up_ref, uscale_ref, down_ref, dscale_ref, had_ref,
     out_ref,
     ring, weights, dring, down, gs, us, ds, had, corner, table, local, tok_row, tok_f32, tok_out, tok, stage, lhs, acc,
-    xsend, xrecv, zbuf, recv_z, rbuf, rot, part, pair_out, pair_in, sums, recv_c,
+    xsend, xrecv, zbuf, recv_z, rbuf, rot, begun, part, pair_out, pair_in, sums, recv_c,
     ring_sem, load_sem, down_sem, tok_ssem, tok_rsem, fwd_ssem, fwd_rsem, x_ssem, x_rsem, z_ssem, z_rsem, r_ssem, r_rsem,
     p_ssem, p_rsem, c_ssem, c_rsem,
 ):
@@ -72,8 +72,15 @@
             device_id=peer, device_id_type=pl.DeviceIdType.MESH,
         )
 
+    def flip(index, mask):
+        out = index
+        for bit in range(mask.bit_length()):
+            if mask >> bit & 1:
+                out = out + (1 - 2 * lax.rem(lax.div(index, 1 << bit), 2)) * (1 << bit)
+        return out
+
     def chip_at(step):
-        return lax.rem(chip + step, chips)
+        return flip(chip, step)
 
     partner = device(mine, chip * 2 + 1 - core)
     peers = [device(mine, lax.rem(me + step, n)) for step in range(1, n)]
@@ -176,7 +183,7 @@
 
     pl.semaphore_wait(barrier, len(peers) + len(across))
 
-    hops = [(d, step) for d in range(groups) for step in range(chips) if (d, step) != (0, 0)]
+    hops = [(d, step) for step in reversed(range(chips)) for d in reversed(range(groups)) if (d, step) != (0, 0)]
 
     def tok_send(p, d, step):
         group = lax.rem(mine + d, groups)
@@ -364,7 +371,7 @@
 
     def r_out(i, count):
         at = pl.ds(0, count)
-        peer = lax.rem(me + i, n)
+        peer = flip(me, i)
         return remote(rbuf.at[peer, at], rot.at[number, at], r_ssem.at[0], r_rsem.at[number], device(mine, peer))
 
     def turn(count):
@@ -384,7 +391,7 @@
                 span *= 2
             for h in range(n):
                 rbuf[h, t] = (cube[h] * scale).astype(bf16)
-        for i in range(1, n):
+        for i in reversed(range(1, n)):
             r_out(i, count).start()
         rot[number] = rbuf[me]
 
@@ -402,16 +409,40 @@
     for c in range(6, down_chunks):
         convert_down(c)
 
-    for o in range(owners):
-
-        @pl.when(me != owner_at(o))
-        def _():
-            count = pl.ds(0, held(o))
-            remote(
-                rbuf.at[0, count], rot.at[o, count], r_ssem.at[0], r_rsem.at[o], device(mine, owner_at(o))
-            ).wait_recv()
-
-    rotated = jnp.concatenate([rot[j % owners, j // owners] for j in range(tiles)], axis=1)
+    def arrived(parity):
+        for o in range(parity, owners, 2):
+
+            @pl.when(me != owner_at(o))
+            def _(o=o):
+                count = pl.ds(0, held(o))
+                remote(
+                    rbuf.at[0, count], rot.at[o, count], r_ssem.at[0], r_rsem.at[o], device(mine, owner_at(o))
+                ).wait_recv()
+
+    side = lax.div(me, n // 2)
+    even = [(o, k) for k in range(rot.shape[1]) for o in range(0, owners, 2) if o + k * owners < tiles]
+    common = [(o, k) for o, k in even if o + 1 + k * owners < tiles]
+    single = [(o, k) for o, k in even if (o, k) not in common]
+
+    def operands(parity, pairs):
+        left = [rot[o + parity, k] for o, k in pairs]
+        rows = [pl.ds(pl.multiple_of((o + k * owners + parity) * LANES, LANES), LANES) for o, k in pairs]
+        return left, rows
+
+    def product(c, left, rows):
+        right = jnp.concatenate([down[c, at, :] for at in rows], axis=0)
+        return jnp.dot(jnp.concatenate(left, axis=1), right, preferred_element_type=f32)
+
+    pl.when(side == 0)(lambda: arrived(0))
+    pl.when(side == 1)(lambda: arrived(1))
+    left, rows = operands(side, common)
+    for c in range(down_chunks):
+        begun[c] = product(c, left, rows)
+    pl.when(side == 0)(lambda: arrived(1))
+    pl.when(side == 1)(lambda: arrived(0))
+    left, rows = operands(1 - side, common)
+    more, more_rows = operands(0, single)
+    left, rows = left + more, rows + more_rows
 
     out_pieces = recv_c.shape[0]
     per_out = down_chunks // out_pieces
@@ -437,13 +468,13 @@
         rows = pl.ds(pl.multiple_of(core * own_rows, own_rows), own_rows)
         both = part[p, rows, :] + pair_in[p].reshape(own_rows, LANES).astype(f32)
         sums[p] = both.astype(bf16).reshape(chips, OUT_ROWS, LANES)
-        for step in range(1, chips):
+        for step in reversed(range(1, chips)):
             c_out(p, step).start()
         recv_c[p, chip] = sums[p, chip]
 
     for p in range(out_pieces):
         for k in range(per_out):
-            res = jnp.dot(rotated, down[p * per_out + k], preferred_element_type=f32)
+            res = begun[p * per_out + k] + product(p * per_out + k, left, rows)
             for b in range(blocks):
                 part[p, pl.ds(k * blocks + b, n, stride=OUT_ROWS), :] = res[:, b * LANES : (b + 1) * LANES]
         pair_out[p] = part[p].astype(bf16).reshape(n, OUT_ROWS, LANES)
@@ -526,6 +557,7 @@
             vmem((n, held, n, LANES), bf16),
             vmem((n, held, n, LANES), bf16),
             vmem((owners, held, n, LANES), bf16),
+            vmem((width // DOWN_COLS, n, DOWN_COLS), f32),
             vmem((out_pieces, n * OUT_ROWS, LANES), f32),
             vmem((out_pieces, n, OUT_ROWS, LANES), bf16),
             vmem((out_pieces, chips, OUT_ROWS, LANES), bf16),

time: 37.9 us -> 36.8 us (0.971)
  Pallas kernels: 36.3 us -> 35.2 us
    pallas_call x1, Pallas kernels: 36.3 us -> 35.2 us  [fused(): pl.pallas_call(functools.partial(kernel, n, groups), out_shape=jax.ShapeD...]
where the time goes in v4:
time: 36.8 us; the launch traced here: 36.6 us
  Pallas kernels  35.2 us (96%)
  local copies, waits for them, and re-layouts  1.41 us (4%)
    pallas_call x1, Pallas kernels, fused(): pl.pallas_call(functools.partial(kernel, n, groups), out_shape=jax.ShapeD...  35.2 us
    unnamed x1, local copies, waits for them, and re-layouts  1.41 us

profile of v4, /device:TPU:0, one launch (start us, length us, event | category | flops | bytes accessed | tf_op | source)
XLA Modules:
  0.0 36.6 jit_solution(16300312915164262050)
XLA Ops:
  0.0 35.2 %shard_map.82 = bf16[1,8192]{1,0:T(2,128)(2,1)} custom-call(bf16[1,8192]{1,0:T(2,128)(2,1)} %tok_ref.1, bf16[8192,1664]{1,0:T(8,128)(2,1)} %gate_ref.1, f32[64,1664]{1,0:T(8,128)} %gscale_ref.1, bf16[8192,1664]{1,0:T(8,128)(2,1)} %up_ref.1, f32[64,1664]{1,0:T(8,128)} %uscale_ref.1, bf16[1664,8192]{1,0:T(8,128)(2,1)} %down_ref.1, f32[1,8192]{1,0:T(1,128)} %bitcast.1, ...), custom_call_target="tpu_custom_call" | custom-call | tf_op jit(solution)/shard_map/pallas_call | solution.py:530
  35.2 1.4 %copy.10 = bf16[1,8192]{1,0:T(2,128)(2,1)} copy(bf16[1,8192]{1,0:T(2,128)(2,1)} %shard_map.82) | data formatting | bytes 32768

commit v5 on v4

--- a/solution.py
+++ b/solution.py
@@ -33,13 +33,12 @@
 LANES = 128
 WIDE = 2 * LANES
 PIECES = 2
-MERGED = 1
 CHUNK = 512
 SLOTS = 6
 DOWN_COLS = 1024
 DOWN_SLOTS = 3
 BLOCK = 64
-OUT_ROWS = 16
+PARTS = (4, 4)
 
 
 def kernel(
@@ -300,24 +299,24 @@
 
     for copy in loads[2:]:
         copy.wait()
-    per_piece = chunks // PIECES
-    last = PIECES - MERGED
-    early = chunks - per_piece
+    early = chunks // PIECES
+
+    def convert_more():
+        for c in range(early, SLOTS):
+            convert(c)
+
     for c in range(early):
         convert(c)
+    pl.when(me < 3 * n // 4)(convert_more)
     relay(0)
-    convert(early)
     relay(1)
-    for p in range(PIECES):
-        ready(p)
-        if p < last:
-            run([p])
-        if p + 2 < PIECES:
-            relay(p + 2)
-        if p == 0:
-            for c in range(early + 1, chunks):
-                convert(c)
-    run(list(range(last, PIECES)))
+    pl.when(me >= 3 * n // 4)(convert_more)
+    ready(0)
+    run([0])
+    for c in range(SLOTS, chunks):
+        convert(c)
+    ready(1)
+    run([1])
 
     for c in range(3):
         convert_down(c)
@@ -444,52 +443,53 @@
     more, more_rows = operands(0, single)
     left, rows = left + more, rows + more_rows
 
-    out_pieces = recv_c.shape[0]
-    per_out = down_chunks // out_pieces
     blocks = DOWN_COLS // LANES
-    own_rows = chips * OUT_ROWS
+    starts = [sum(PARTS[:p]) for p in range(len(PARTS))]
+    own_rows = [chips * size * blocks for size in PARTS]
 
     def pair_copy(p, which):
         at = pl.ds(which * chips, chips)
-        return remote(pair_out.at[p, at], pair_in.at[p], p_ssem.at[p], p_rsem.at[p], partner)
+        return remote(pair_out[p].at[at], pair_in[p], p_ssem.at[p], p_rsem.at[p], partner)
 
     def c_out(p, step):
         to = chip_at(step)
         return remote(
-            sums.at[p, to], recv_c.at[p, chip], c_ssem.at[p], c_rsem.at[p], device(mine, to * 2 + core)
+            sums[p].at[to], recv_c[p].at[chip], c_ssem.at[p], c_rsem.at[p], device(mine, to * 2 + core)
         )
 
     def c_all(p, ref):
-        at = ref.at[p, pl.ds(0, chips - 1)]
+        at = ref.at[pl.ds(0, chips - 1)]
         return remote(at, at, c_ssem.at[p], c_rsem.at[p], partner)
 
     def finish(p):
         pair_copy(p, core).wait_recv()
-        rows = pl.ds(pl.multiple_of(core * own_rows, own_rows), own_rows)
-        both = part[p, rows, :] + pair_in[p].reshape(own_rows, LANES).astype(f32)
-        sums[p] = both.astype(bf16).reshape(chips, OUT_ROWS, LANES)
+        rows = pl.ds(pl.multiple_of(core * own_rows[p], own_rows[p]), own_rows[p])
+        both = part[p][rows, :] + pair_in[p][...].reshape(own_rows[p], LANES).astype(f32)
+        sums[p][...] = both.astype(bf16).reshape(sums[p].shape)
         for step in reversed(range(1, chips)):
             c_out(p, step).start()
-        recv_c[p, chip] = sums[p, chip]
-
-    for p in range(out_pieces):
-        for k in range(per_out):
-            res = begun[p * per_out + k] + product(p * per_out + k, left, rows)
+        recv_c[p][chip] = sums[p][chip]
+
+    for p, size in enumerate(PARTS):
+        for k in range(size):
+            c = starts[p] + k
+            res = begun[c] + product(c, left, rows)
             for b in range(blocks):
-                part[p, pl.ds(k * blocks + b, n, stride=OUT_ROWS), :] = res[:, b * LANES : (b + 1) * LANES]
-        pair_out[p] = part[p].astype(bf16).reshape(n, OUT_ROWS, LANES)
+                part[p][pl.ds(k * blocks + b, n, stride=size * blocks), :] = res[:, b * LANES : (b + 1) * LANES]
+        pair_out[p][...] = part[p][...].astype(bf16).reshape(pair_out[p].shape)
         pair_copy(p, 1 - core).start()
         if p > 0:
             finish(p - 1)
-    finish(out_pieces - 1)
-
-    for p in range(out_pieces):
-        c_all(p, recv_c).wait_recv()
-        total = recv_c[p, 0].astype(f32)
+    finish(len(PARTS) - 1)
+
+    for p, size in enumerate(PARTS):
+        c_all(p, recv_c[p]).wait_recv()
+        total = recv_c[p][0].astype(f32)
         for h in range(1, chips):
-            total = total + recv_c[p, h].astype(f32)
-        for r in range(OUT_ROWS):
-            cols = slice((p * OUT_ROWS + r) * LANES, (p * OUT_ROWS + r + 1) * LANES)
+            total = total + recv_c[p][h].astype(f32)
+        for r in range(size * blocks):
+            at = (starts[p] * blocks + r) * LANES
+            cols = slice(at, at + LANES)
             out_ref[:, cols] = (total[r : r + 1, :] * ds[:, cols]).astype(out_ref.dtype)
 
     for p in range(PIECES):
@@ -508,9 +508,9 @@
         remote(every, every, r_ssem.at[0], r_rsem.at[0], partner).wait_send()
 
     by_count(drain)
-    for p in range(out_pieces):
+    for p in range(len(PARTS)):
         pair_copy(p, 1 - core).wait_send()
-        c_all(p, sums).wait_send()
+        c_all(p, sums[p]).wait_send()
 
 
 def fused(n, groups, tokens, gate_codes, gate_scales, up_codes, up_scales, down_codes, down_scales, hadamard):
@@ -519,7 +519,7 @@
     tiles = units // LANES
     piece_rows = depth // (groups * PIECES * LANES)
     half_scales = (gate_scales.shape[0] // groups, units)
-    out_pieces = width // (LANES * OUT_ROWS)
+    rows = DOWN_COLS // LANES
     owners = n // 2
     held = -(-tiles // owners)
     spans = -(-units // WIDE)
@@ -558,11 +558,11 @@
             vmem((n, held, n, LANES), bf16),
             vmem((owners, held, n, LANES), bf16),
             vmem((width // DOWN_COLS, n, DOWN_COLS), f32),
-            vmem((out_pieces, n * OUT_ROWS, LANES), f32),
-            vmem((out_pieces, n, OUT_ROWS, LANES), bf16),
-            vmem((out_pieces, chips, OUT_ROWS, LANES), bf16),
-            vmem((out_pieces, chips, OUT_ROWS, LANES), bf16),
-            vmem((out_pieces, chips, OUT_ROWS, LANES), bf16),
+            tuple(vmem((n * size * rows, LANES), f32) for size in PARTS),
+            tuple(vmem((n, size * rows, LANES), bf16) for size in PARTS),
+            tuple(vmem((chips, size * rows, LANES), bf16) for size in PARTS),
+            tuple(vmem((chips, size * rows, LANES), bf16) for size in PARTS),
+            tuple(vmem((chips, size * rows, LANES), bf16) for size in PARTS),
             dma((SLOTS,)),
             dma((5,)),
             dma((DOWN_SLOTS,)),
@@ -576,10 +576,10 @@
             dma((1,)),
             dma((1,)),
             dma((owners,)),
-            dma((out_pieces,)),
-            dma((out_pieces,)),
-            dma((out_pieces,)),
-            dma((out_pieces,)),
+            dma((len(PARTS),)),
+            dma((len(PARTS),)),
+            dma((len(PARTS),)),
+            dma((len(PARTS),)),
         ],
         compiler_params=pltpu.CompilerParams(
             collective_id=0, has_side_effects=True, vmem_limit_bytes=67043328
@@ -606,7 +606,7 @@
         and depth == scale_rows * LANES
         and scale_rows % (groups * PIECES * 8) == 0
         and depth == 8 * groups * CHUNK
-        and width == 8 * DOWN_COLS
+        and width == sum(PARTS) * DOWN_COLS
         and units % LANES == 0
         and n // 2 <= units // LANES <= n
     )

time: 36.8 us -> 36.1 us (0.981)
  Pallas kernels: 35.2 us -> 34.5 us
    pallas_call x1, Pallas kernels: 35.2 us -> 34.5 us  [fused(): pl.pallas_call(functools.partial(kernel, n, groups), out_shape=jax.ShapeD...]
where the time goes in v5:
time: 36.1 us; the launch traced here: 35.9 us
  Pallas kernels  34.5 us (96%)
  local copies, waits for them, and re-layouts  1.41 us (4%)
    pallas_call x1, Pallas kernels, fused(): pl.pallas_call(functools.partial(kernel, n, groups), out_shape=jax.ShapeD...  34.5 us
    unnamed x1, local copies, waits for them, and re-layouts  1.41 us

profile of v5, /device:TPU:0, one launch (start us, length us, event | category | flops | bytes accessed | tf_op | source)
XLA Modules:
  0.0 35.9 jit_solution(9361819911351724882)
XLA Ops:
  0.0 34.5 %shard_map.82 = bf16[1,8192]{1,0:T(2,128)(2,1)} custom-call(bf16[1,8192]{1,0:T(2,128)(2,1)} %tok_ref.1, bf16[8192,1664]{1,0:T(8,128)(2,1)} %gate_ref.1, f32[64,1664]{1,0:T(8,128)} %gscale_ref.1, bf16[8192,1664]{1,0:T(8,128)(2,1)} %up_ref.1, f32[64,1664]{1,0:T(8,128)} %uscale_ref.1, bf16[1664,8192]{1,0:T(8,128)(2,1)} %down_ref.1, f32[1,8192]{1,0:T(1,128)} %bitcast.1, ...), custom_call_target="tpu_custom_call" | custom-call | tf_op jit(solution)/shard_map/pallas_call | solution.py:530
  34.5 1.4 %copy.10 = bf16[1,8192]{1,0:T(2,128)(2,1)} copy(bf16[1,8192]{1,0:T(2,128)(2,1)} %shard_map.82) | data formatting | bytes 32768

commit v6 on v5

--- a/solution.py
+++ b/solution.py
@@ -274,10 +274,11 @@
         return sums_now
 
     spans = [(at, min(WIDE, units - at)) for at in range(0, units, WIDE)]
+    wide_tiles = WIDE // LANES
 
     def x_send(j, width):
-        at = (j, slice(None), slice(None), pl.ds(0, width))
-        return remote(xsend.at[at], xrecv.at[at], x_ssem.at[j], x_rsem.at[j], across[0])
+        at = pl.ds(j * wide_tiles, width // LANES)
+        return remote(xsend.at[at], xrecv.at[at], x_ssem.at[0], x_rsem.at[j], across[0])
 
     def run(pieces):
         final = pieces[-1] + 1 == PIECES
@@ -293,7 +294,8 @@
                 else:
                     total = acc[w, :, cols] + pair[w]
                     acc[w, :n, cols] = total[:n]
-                    xsend[j, w, :, :width] = total[n:].astype(bf16)
+                    for t in range(width // LANES):
+                        xsend[j * wide_tiles + t, w] = total[n:, t * LANES : (t + 1) * LANES].astype(bf16)
             if final:
                 x_send(j, width).start()
 
@@ -324,8 +326,11 @@
     for j, (at, width) in enumerate(spans):
         x_send(j, width).wait_recv()
         cols = slice(at, at + width)
-        gate = acc[0, :n, cols] + xrecv[j, 0, :, :width].astype(f32)
-        lift = acc[1, :n, cols] + xrecv[j, 1, :, :width].astype(f32)
+        gate, lift = [
+            acc[w, :n, cols]
+            + jnp.concatenate([xrecv[j * wide_tiles + t, w] for t in range(width // LANES)], axis=1).astype(f32)
+            for w in range(2)
+        ]
         hidden = (gate / (1.0 + jnp.exp(-gate)) * lift).astype(bf16)
         new = jnp.dot(hidden, local[cols, :], preferred_element_type=f32)
         turned = new if turned is None else turned + new
@@ -495,8 +500,7 @@
     for p in range(PIECES):
         tok_all(p).wait_send()
         forward(p, core).wait_send()
-    for j, (at, width) in enumerate(spans):
-        x_send(j, width).wait_send()
+    remote(xsend, xrecv, x_ssem.at[0], x_rsem.at[0], across[0]).wait_send()
     for o in range(owners):
 
         @pl.when(me != owner_at(o))
@@ -551,8 +555,8 @@
             vmem((2 * n * piece_rows, LANES), f32),
             vmem((PIECES, piece_rows // 2, 4 * n, WIDE), bf16),
             vmem((2, 2 * n, units), f32),
-            vmem((spans, 2, n, WIDE), bf16),
-            vmem((spans, 2, n, WIDE), bf16),
+            vmem((tiles, 2, n, LANES), bf16),
+            vmem((tiles, 2, n, LANES), bf16),
             vmem((owners, held, n, LANES), bf16),
             vmem((n, held, n, LANES), bf16),
             vmem((n, held, n, LANES), bf16),
@@ -570,7 +574,7 @@
             dma((PIECES,)),
             dma((PIECES,)),
             dma((PIECES,)),
-            dma((spans,)),
+            dma((1,)),
             dma((spans,)),
             dma((owners,)),
             dma((1,)),

time: 36.1 us -> 36 us (level)
  no operation moved by 1% of the time
where the time goes in v6:
time: 36 us; the launch traced here: 35.9 us
  Pallas kernels  34.5 us (96%)
  local copies, waits for them, and re-layouts  1.41 us (4%)
    pallas_call x1, Pallas kernels, fused(): pl.pallas_call(functools.partial(kernel, n, groups), out_shape=jax.ShapeD...  34.5 us
    unnamed x1, local copies, waits for them, and re-layouts  1.41 us

profile of v6, /device:TPU:0, one launch (start us, length us, event | category | flops | bytes accessed | tf_op | source)
XLA Modules:
  0.0 35.9 jit_solution(5289969820283520637)
XLA Ops:
  0.0 34.5 %shard_map.82 = bf16[1,8192]{1,0:T(2,128)(2,1)} custom-call(bf16[1,8192]{1,0:T(2,128)(2,1)} %tok_ref.1, bf16[8192,1664]{1,0:T(8,128)(2,1)} %gate_ref.1, f32[64,1664]{1,0:T(8,128)} %gscale_ref.1, bf16[8192,1664]{1,0:T(8,128)(2,1)} %up_ref.1, f32[64,1664]{1,0:T(8,128)} %uscale_ref.1, bf16[1664,8192]{1,0:T(8,128)(2,1)} %down_ref.1, f32[1,8192]{1,0:T(1,128)} %bitcast.1, ...), custom_call_target="tpu_custom_call" | custom-call | tf_op jit(solution)/shard_map/pallas_call | solution.py:534
  34.5 1.4 %copy.10 = bf16[1,8192]{1,0:T(2,128)(2,1)} copy(bf16[1,8192]{1,0:T(2,128)(2,1)} %shard_map.82) | data formatting | bytes 32768
